TPU v7x, 512 devices: a whole 4x8x8 slice. The times are simulated.
512 devices in a mesh: region: 16 (over z, core), dev: 32 (over y, x).
Axes of the slice: x: 4, y: 8, z: 8, core: 2. Of those that a mesh axis runs over, the one named last changes fastest.
Arguments:
- basis_values: bfloat16 [6144, 4, 256, 128], P(('region', 'dev')), may hold values from -6 to 6
- density_rows: bfloat16 [1536, 4, 128, 128], P(('region', 'dev')), may hold values from -0.013671875 to 0.013671875
- block_mask: int32 [1536, 4], P(('region', 'dev')), may hold values 0 or 1
- window_start: int32 [512], P(('region', 'dev')), may hold values from 0 to 95
- batch_offsets: int32 [512, 12], P(('region', 'dev')), may hold values from 0 to 28, as said below
- batch_sizes: int32 [512, 12], P(('region', 'dev')), may hold values from 1 to 256, 1920 in all within a row
- atom_near: int32 [6144, 6], P(('region', 'dev')), may hold values from 0 to 1535
- harmonics: bfloat16 [6144, 6, 25, 256], P(('region', 'dev')), may hold values from -6 to 6
- partition: float32 [6144, 6, 256], P(('region', 'dev')), may hold values from 0.002 to 0.05
- radius: float32 [6144, 6, 256], P(('region', 'dev')), may hold values from 0 to 15
- radial_table: float32 [25, 16], replicated, may hold values from -1.5 to 1.5
Outputs:
- density: float32 [6144, 256], P(('region', 'dev'))
- moments: float32 [25, 8192], P(None, ('region', 'dev'))
- potential: float32 [6144, 256], P(('region', 'dev'))
Inputs may be any that keep to these rules, and one draw needn't show every extreme that they name: The blocks of a batch are positions batch_offsets to batch_offsets + 3 of its device's window of 32 consecutive blocks.
All inputs are finite; a program needn't handle non-finite values. No bound on the sum of `block_mask` on one device may be relied on, other than what follows from the above.
Results may differ from a plain program's by a relative error of at most 0.0029.
Values may be sent and summed in bfloat16 or wider, within the bound.
A program may use at most 64 MiB of HBM per device.

v0:
```python
import jax
import jax.numpy as jnp
from jax import lax
from jax.sharding import PartitionSpec as P

ATOM_DEV = 16


def padded_2(cells, sides, width):
    for axis, dim in sides:
        count = lax.axis_size(axis)
        head = lax.slice_in_dim(cells, 0, width, axis=dim)
        tail = lax.slice_in_dim(cells, cells.shape[dim] - width, cells.shape[dim], axis=dim)
        cells = jnp.concatenate(
            [
                lax.ppermute(tail, axis, [(i, (i + 1) % count) for i in range(count)]),
                cells,
                lax.ppermute(head, axis, [((i + 1) % count, i) for i in range(count)]),
            ],
            axis=dim,
        )
    return cells


def spline_basis(radii_row, knot_count):
    knot_points = jnp.arange(knot_count).astype(jnp.float32)
    distance = jnp.abs(radii_row[..., None, :] - knot_points[:, None])
    inner_part = 2.0 / 3.0 - distance * distance + 0.5 * distance * distance * distance
    remote = 2.0 - distance
    outer_part = remote * remote * remote / 6.0
    return jnp.where(distance < 1.0, inner_part, jnp.where(distance < 2.0, outer_part, 0.0))


def batch_density(values, row_blocks):
    block_total = values.shape[0]
    band_width = row_blocks.shape[1]
    leading = jnp.zeros((1,) + values.shape[1:], values.dtype)
    trailing = jnp.zeros((band_width - 2,) + values.shape[1:], values.dtype)
    padded = jnp.concatenate([leading, values, trailing], axis=0)
    stacked = jnp.stack(
        [padded[column : column + block_total] for column in range(band_width)], axis=2
    )
    mixed_rows = jnp.einsum(
        "jpkf,jkgf->jpg", stacked, row_blocks, preferred_element_type=jnp.float32
    )
    return jnp.sum(values.astype(jnp.float32) * mixed_rows, axis=(0, 2))


def per_device(
    basis_values,
    density_rows,
    block_mask,
    window_start,
    batch_offsets,
    batch_sizes,
    atom_near,
    harmonics,
    partition,
    radius,
    radial_table,
):
    dev_count = lax.axis_size("dev")
    blocks_dev = density_rows.shape[0]
    block_count = blocks_dev * dev_count
    masked = density_rows * block_mask.astype(jnp.bfloat16)[:, :, None, None]
    first_block = window_start[0]
    positions = jnp.arange(dev_count, dtype=jnp.int32)
    spatial = (first_block + positions) % block_count
    owner_index = spatial % dev_count
    slot_index = spatial // dev_count
    stored = owner_index * blocks_dev + slot_index
    empty_rows = jnp.zeros((dev_count,) + masked.shape[1:], jnp.bfloat16)
    shard_rows = lax.all_gather(masked, "dev", axis=0, tiled=True)
    inside = (stored >= 0) & (stored < shard_rows.shape[0])
    chosen = jnp.take(shard_rows, jnp.clip(stored, 0, shard_rows.shape[0] - 1), axis=0)
    window = jnp.where(inside[:, None, None, None], chosen, empty_rows)

    def one_density(batch_item):
        values, offset = batch_item
        row_blocks = lax.dynamic_slice_in_dim(window, offset, values.shape[0], 0)
        return batch_density(values, row_blocks)

    point_total = basis_values.shape[2]
    alive_mask = (
        jnp.arange(point_total, dtype=jnp.int32)[None, :] < batch_sizes[0][:, None]
    ).astype(jnp.float32)
    density = lax.map(one_density, (basis_values, batch_offsets[0])) * alive_mask
    moment_terms = jnp.einsum(
        "bip,bilp->bil",
        partition * density[:, None, :],
        harmonics.astype(jnp.float32),
        precision=lax.Precision.HIGHEST,
    )
    comp_total = moment_terms.shape[2]
    atom_region = ATOM_DEV * dev_count
    flattened = atom_near.reshape(-1)
    onehot = (flattened[:, None] == jnp.arange(3 * atom_region, dtype=jnp.int32)[None, :]).astype(
        jnp.float32
    )
    partial_value = jnp.dot(
        moment_terms.reshape(-1, comp_total).T, onehot, precision=lax.Precision.HIGHEST
    )
    partial_value = partial_value.reshape(comp_total, 3, atom_region).transpose(1, 0, 2)
    owner_sums = lax.psum_scatter(partial_value, "dev", scatter_dimension=2, tiled=True)
    side_parts = jnp.stack([owner_sums[0], owner_sums[2]])[None]
    rim_parts = padded_2(side_parts, (("region", 0),), 1)
    moments = owner_sums[1] + rim_parts[0, 1] + rim_parts[2, 0]
    own_table = (moments[:, None, :] * radial_table[:, :, None]).astype(jnp.bfloat16)
    rim_table = padded_2(own_table[None], (("region", 0),), 1)
    spline_table = lax.all_gather(rim_table, "dev", axis=3, tiled=True)
    knot_total = radial_table.shape[1]
    batch_total = atom_near.shape[0]
    near_total = atom_near.shape[1]
    table_flat = spline_table.transpose(1, 2, 0, 3).reshape(comp_total, knot_total, 3 * atom_region)
    selected = jnp.take(table_flat, flattened, axis=2).reshape(
        comp_total, knot_total, batch_total, near_total
    )
    spline = spline_basis(radius, knot_total)
    radial = jnp.einsum(
        "lrbi,birp->bilp", selected.astype(jnp.float32), spline, precision=lax.Precision.HIGHEST
    )
    potential = jnp.sum(harmonics.astype(jnp.float32) * radial, axis=(1, 2)) * alive_mask
    return (density, moments, potential)


def solution(mesh):
    placed = (
        P(("region", "dev"), None, None, None),
        P(("region", "dev"), None, None, None),
        P(("region", "dev"), None),
        P(("region", "dev")),
        P(("region", "dev"), None),
        P(("region", "dev"), None),
        P(("region", "dev"), None),
        P(("region", "dev"), None, None, None),
        P(("region", "dev"), None, None),
        P(("region", "dev"), None, None),
        P(),
    )
    return jax.shard_map(
        per_device,
        mesh=mesh,
        in_specs=placed,
        out_specs=(
            P(("region", "dev"), None),
            P(None, ("region", "dev")),
            P(("region", "dev"), None),
        ),
        check_vma=False,
    )
```

profile of v0, /device:TPU:1, one launch (start us, length us, event | category | flops | bytes accessed | tf_op | source)
XLA Modules:
  0.0 500.1 jit_solution(12459849883825730145)
XLA Ops:
  7.2 0.7 convert_element_type.30
  7.9 1.9 broadcast_multiply_fusion
  10.8 130.3 %all-gather.3.cloned.1.call-done = bf16[96,4,128,128]{3,2,1,0:T(8,128)(2,1)} async-done(((bf16[3,4,128,128]{3,2,1,0:T(8,128)(2,1)}), bf16[96,4,128,128]{3,2,1,0:T(8,128)(2,1)}) %all-gather.3.cloned.1.call-update) | async-done | bytes 12582928 | tf_op jit(solution)/shard_map/all_gather | solution.py:73
  141.0 7.6 %gather_fusion = bf16[32,4,128,128]{3,2,1,0:T(8,128)(2,1)} fusion(bf16[96,4,128,128]{3,2,1,0:T(8,128)(2,1)} %all-gather.3.cloned.1.call-done, s32[1024]{0:T(1024)S(1)} %pad_clamp_fusion.1), kind=kCustom, calls=%fused_computation | custom fusion | bytes 8388736 | tf_op jit(solution)/shard_map/jit(_take)/gather | solution.py:75
  148.6 4.7 select_select_fusion
  153.3 63.6 %while.11 = (s32[]{:T(128)}, f32[12,256]{1,0:T(8,128)S(1)}, bf16[12,4,256,128]{3,2,1,0:T(8,128)(2,1)}, s32[12]{0:T(128)S(1)}, bf16[32,4,128,128]{3,2,1,0:T(8,128)(2,1)}) while((s32[]{:T(128)}, f32[12,256]{1,0:T(8,128)S(1)}, bf16[12,4,256,128]{3,2,1,0:T(8,128)(2,1)}, s32[12]{0:T(128)S(1)}, bf16[32,4,128,128]{3,2,1,0:T(8,128)(2,1)}) %tuple.48), condition=%wide.region_2.3_spmd.clone, body=%wide.region_0.2_spmd.sunk.clone | while | flops 136183552 | bytes 3673207 | solution.py:87
  155.8 1.0 dynamic-slice_bitcast_fusion.4
  157.0 1.6 fusion.73
  161.1 1.0 dynamic-slice_bitcast_fusion.4
  162.3 1.6 fusion.73
  166.4 1.0 dynamic-slice_bitcast_fusion.4
  167.6 1.6 fusion.73
  171.7 1.0 dynamic-slice_bitcast_fusion.4
  172.9 1.6 fusion.73
  177.0 1.0 dynamic-slice_bitcast_fusion.4
  178.2 1.6 fusion.73
  182.3 1.0 dynamic-slice_bitcast_fusion.4
  183.5 1.6 fusion.73
  187.6 1.0 dynamic-slice_bitcast_fusion.4
  188.8 1.6 fusion.73
  192.9 1.0 dynamic-slice_bitcast_fusion.4
  194.1 1.6 fusion.73
  198.2 1.0 dynamic-slice_bitcast_fusion.4
  199.3 1.6 fusion.73
  203.5 1.0 dynamic-slice_bitcast_fusion.4
  204.6 1.6 fusion.73
  208.8 1.0 dynamic-slice_bitcast_fusion.4
  209.9 1.6 fusion.73
  214.1 1.0 dynamic-slice_bitcast_fusion.4
  215.2 1.6 fusion.73
  217.0 1.0 fusion.41
  218.4 1.4 copy.37
  219.8 1.3 dynamic-slice
  221.7 152.0 %all-reduce.5.cloned.1.call-done = f32[3,25,512]{1,0,2:T(4,128)} async-done(((f32[3,25,512]{1,0,2:T(4,128)}), f32[3,25,512]{1,0,2:T(4,128)}) %all-reduce.5.cloned.1.call-update) | async-done | bytes 153616
  373.7 0.9 constant_dynamic-slice_fusion.1
  374.7 5.2 %collective-permute-start.1 = (f32[1,2,25,16]{2,1,3,0:T(2,128)S(1)}, f32[1,2,25,16]{2,1,3,0:T(2,128)S(1)}, u32[]{:S(2)}, u32[]{:S(2)}) collective-permute-start(f32[1,2,25,16]{2,1,3,0:T(2,128)S(1)} %maximum_bitcast_fusion), channel_id=1, source_target_pairs={{32,0},{64,32},{96,64},{128,96},{160,128},{192,160},{224,192},{256... | collective-permute-start | bytes 9608 | tf_op jit(solution)/shard_map/ppermute | solution.py:18
  379.9 1.3 collective-permute-start
  381.1 1.4 collective-permute-done.1
  382.6 1.8 collective-permute-start.2
  384.4 1.1 collective-permute-start.3
  385.4 0.7 collective-permute-done.2
  386.2 1.9 collective-permute-done.3
  388.1 0.7 copy.41
  389.1 91.7 %all-gather.5.cloned.1.call-done = bf16[3,25,16,512]{1,2,0,3:T(8,128)(2,1)} async-done(((bf16[3,25,16,16]{1,2,0,3:T(8,128)(2,1)}), bf16[3,25,16,512]{1,2,0,3:T(8,128)(2,1)}) %all-gather.5.cloned.1.call-update) | async-done | bytes 1228816 | tf_op jit(solution)/shard_map/all_gather | solution.py:110
  480.7 6.5 %copy.51 = bf16[25,16,3,512]{0,1,3,2:T(8,128)(2,1)} copy(bf16[25,16,3,512]{0,1,2,3:T(8,128)(2,1)} %bitcast.76) | data formatting | bytes 2457600 | tf_op jit(solution)/shard_map/reshape | solution.py:114
  487.3 3.4 gather_fusion.1
  490.7 2.2 multiply_reduce_fusion
  492.9 0.7 fusion.44
  (85 shorter events, 10.0 us)
Async XLA Ops:
  7.2 3.3 copy-start.3
  7.2 133.9 %all-gather.3.cloned.1.call-start = ((), (), s32[]{:S(2)}) async-start(), calls=%async_computation | async-start | bytes 12976128 | tf_op jit(solution)/shard_map/all_gather | solution.py:73
  9.8 363.9 %all-reduce.5.cloned.1.call-start = ((), (), s32[]{:S(2)}) async-start(), calls=%async_computation.2 | async-start | bytes 2097152
  148.6 4.7 copy-start.8
  153.3 63.6 %copy-start.5 = (s32[1,12]{1,0:T(1,128)S(1)}, s32[1,12]{1,0:T(1,128)}, u32[]{:S(2)}) copy-start(s32[1,12]{1,0:T(1,128)} %param.18) | copy-start | bytes 148
  153.3 63.7 %copy-start = (f32[12,6,256]{2,1,0:T(8,128)S(1)}, f32[12,6,256]{2,1,0:T(8,128)}, u32[]{:S(2)}) copy-start(f32[12,6,256]{2,1,0:T(8,128)} %param.21) | copy-start | bytes 221188
  153.3 63.7 %copy-start.6 = (bf16[12,6,25,256]{3,2,1,0:T(8,128)(2,1)S(1)}, bf16[12,6,25,256]{3,2,1,0:T(8,128)(2,1)}, u32[]{:S(2)}) copy-start(bf16[12,6,25,256]{3,2,1,0:T(8,128)(2,1)} %param.20) | copy-start | bytes 2764804
  216.9 2.8 copy-start.1
  218.4 164.2 %copy-start.4 = (f32[25,16]{0,1:T(8,128)S(1)}, f32[25,16]{0,1:T(8,128)}, u32[]{:S(2)}) copy-start(f32[25,16]{0,1:T(8,128)} %param.23) | copy-start | bytes 4804
  219.8 261.0 %all-gather.5.cloned.1.call-start = ((), (), s32[]{:S(2)}) async-start(), calls=%async_computation.1 | async-start | bytes 6488064 | tf_op jit(solution)/shard_map/all_gather | solution.py:110
  374.7 7.9 %collective-permute-start.1 = (f32[1,2,25,16]{2,1,3,0:T(2,128)S(1)}, f32[1,2,25,16]{2,1,3,0:T(2,128)S(1)}, u32[]{:S(2)}, u32[]{:S(2)}) collective-permute-start(f32[1,2,25,16]{2,1,3,0:T(2,128)S(1)} %maximum_bitcast_fusion), channel_id=1, source_target_pairs={{32,0},{64,32},{96,64},{128,96},{160,128},{192,160},{224,192},{256... | collective-permute-start | bytes 9608 | tf_op jit(solution)/shard_map/ppermute | solution.py:18
  379.9 2.7 collective-permute-start
  382.6 104.7 %copy-start.2 = (f32[25,16]{0,1:T(8,128)}, f32[25,16]{0,1:T(8,128)S(1)}, u32[]{:S(2)}) copy-start(f32[25,16]{0,1:T(8,128)S(1)} %fusion.47) | copy-start | bytes 4804
  382.6 3.5 collective-permute-start.2
  384.4 3.7 collective-permute-start.3
  480.7 10.0 %copy-start.7 = (f32[12,6,256]{2,1,0:T(8,128)S(1)}, f32[12,6,256]{2,1,0:T(8,128)}, u32[]{:S(2)}) copy-start(f32[12,6,256]{2,1,0:T(8,128)} %param.22) | copy-start | bytes 221188
Sparse Core Ops, SparseCore 0:
  11.2 129.8 all-gather.2
  219.9 153.7 all-reduce.4
  389.0 91.7 all-gather.4
where the time goes:
time: 502 us; the launch traced here: 500 us
  waiting for transfers between devices  378 us (75%)
  local copies, waits for them, and re-layouts  43.2 us (9%)
  loops' own time  23.7 us (5%)
  matrix products  22.4 us (4%)
  between operations  15.2 us (3%)
  starting transfers between devices  9.43 us (2%)
  other arithmetic  8.16 us (2%)
    unnamed x4, waiting for transfers between devices  152 us
    all_gather x1, waiting for transfers between devices, per_device(): shard_rows = lax.all_gather(masked, 'dev', axis=0, tiled=True)  130 us
    all_gather x1, waiting for transfers between devices, per_device(): spline_table = lax.all_gather(rim_table, 'dev', axis=3, tiled=True)  91.7 us
    another operation x1, loops' own time, per_device(): lax.map(one_density, (basis_values, batch_offsets[0])) * alive_mask  23.7 us
    dot_general x12, matrix products, batch_density(): jnp.einsum('jpkf,jkgf->jpg', stacked, row_blocks, preferred_element_type=...  18.8 us
    another operation x24, local copies, waits for them, and re-layouts, batch_density(): jnp.stack([padded[column:column + block_total] for column in range(band_w...  13.5 us
  transfers between devices with their start and end apart: 7, of which 6 were waited for; matrix products, arithmetic and copies ran while one was open for 0% of the time, Pallas kernels for 0%

commit v1 on v0

--- a/solution.py
+++ b/solution.py
@@ -2,6 +2,7 @@
 import jax.numpy as jnp
 from jax import lax
 from jax.sharding import PartitionSpec as P
+from jax.lax import all_to_all, axis_size
 
 ATOM_DEV = 16
 
@@ -70,7 +71,9 @@
     slot_index = spatial // dev_count
     stored = owner_index * blocks_dev + slot_index
     empty_rows = jnp.zeros((dev_count,) + masked.shape[1:], jnp.bfloat16)
-    shard_rows = lax.all_gather(masked, "dev", axis=0, tiled=True)
+    fresh = jnp.stack([masked for _ in range(axis_size("dev"))])
+    plain = all_to_all(fresh, "dev", 0, 0)
+    shard_rows = jnp.concatenate(plain, 0)
     inside = (stored >= 0) & (stored < shard_rows.shape[0])
     chosen = jnp.take(shard_rows, jnp.clip(stored, 0, shard_rows.shape[0] - 1), axis=0)
     window = jnp.where(inside[:, None, None, None], chosen, empty_rows)

time: 502 us -> 696 us (1.39)
  waiting for transfers between devices: 378 us -> 554 us
  starting transfers between devices: 9.43 us -> 20.1 us
  local copies, waits for them, and re-layouts: 43.2 us -> 50.9 us
    all_to_all x0 -> x1, waiting for transfers between devices: none -> 278 us  [per_device(): plain = all_to_all(fresh, 'dev', 0, 0)]
    all_gather x1 -> x0, waiting for transfers between devices: 130 us -> none  [per_device(): shard_rows = lax.all_gather(masked, 'dev', axis=0, tiled=True)]
    unnamed x4 -> x3, waiting for transfers between devices: 152 us -> 181 us
    all_to_all x0 -> x1, starting transfers between devices: none -> 10.7 us  [per_device(): plain = all_to_all(fresh, 'dev', 0, 0)]
    another operation x0 -> x1, local copies, waits for them, and re-layouts: none -> 7.68 us  [per_device(): fresh = jnp.stack([masked for _ in range(axis_size('dev'))])]
where the time goes in v1:
time: 696 us; the launch traced here: 694 us
  waiting for transfers between devices  554 us (80%)
  local copies, waits for them, and re-layouts  50.9 us (7%)
  loops' own time  23.7 us (3%)
  matrix products  22.4 us (3%)
  starting transfers between devices  20.1 us (3%)
  between operations  15.5 us (2%)
  other arithmetic  7.39 us (1%)
    all_to_all x1, waiting for transfers between devices, per_device(): plain = all_to_all(fresh, 'dev', 0, 0)  278 us
    unnamed x3, waiting for transfers between devices  181 us
    all_gather x1, waiting for transfers between devices, per_device(): spline_table = lax.all_gather(rim_table, 'dev', axis=3, tiled=True)  91.7 us
    another operation x1, loops' own time, per_device(): lax.map(one_density, (basis_values, batch_offsets[0])) * alive_mask  23.7 us
    dot_general x12, matrix products, batch_density(): jnp.einsum('jpkf,jkgf->jpg', stacked, row_blocks, preferred_element_type=...  18.8 us
  transfers between devices with their start and end apart: 7, of which 6 were waited for; matrix products, arithmetic and copies ran while one was open for 0% of the time, Pallas kernels for 0%

profile of v1, /device:TPU:1, one launch (start us, length us, event | category | flops | bytes accessed | tf_op | source)
XLA Modules:
  0.0 694.4 jit_solution(3562708238274735685)
XLA Ops:
  7.8 1.1 broadcast_multiply_fusion
  8.9 7.7 %stack.14 = bf16[32,3,4,128,128]{4,3,2,1,0:T(8,128)(2,1)} broadcast(bf16[3,4,128,128]{3,2,1,0:T(8,128)(2,1)S(1)} %broadcast_multiply_fusion), dimensions={1,2,3,4} | broadcast | bytes 12976128 | tf_op jit(solution)/shard_map/stack | solution.py:74
  16.6 10.7 %all-to-all-start = ((bf16[32,3,4,128,128]{4,3,2,1,0:T(8,128)(2,1)}), bf16[32,3,4,128,128]{4,3,2,1,0:T(8,128)(2,1)}, u32[]{:S(2)}, u32[]{:S(2)}) async-start(bf16[32,3,4,128,128]{4,3,2,1,0:T(8,128)(2,1)} %stack.14), calls=%async_computation | async-start | bytes 25165824 | tf_op jit(solution)/shard_map/all_to_all | solution.py:75
  28.4 278.1 %all-to-all-done = bf16[32,3,4,128,128]{4,3,2,1,0:T(8,128)(2,1)} async-done(((bf16[32,3,4,128,128]{4,3,2,1,0:T(8,128)(2,1)}), bf16[32,3,4,128,128]{4,3,2,1,0:T(8,128)(2,1)}, u32[]{:S(2)}, u32[]{:S(2)}) %all-to-all-start) | async-done | bytes 12582944 | tf_op jit(solution)/shard_map/all_to_all | solution.py:75
  306.4 7.6 %gather_fusion = bf16[32,4,128,128]{3,2,1,0:T(8,128)(2,1)} fusion(bf16[96,4,128,128]{3,2,1,0:T(8,128)(2,1)} %bitcast.13, s32[1024]{0:T(1024)S(1)} %pad_clamp_fusion.1), kind=kCustom, calls=%fused_computation | custom fusion | bytes 8388736 | tf_op jit(solution)/shard_map/jit(_take)/gather | solution.py:78
  314.0 4.7 select_select_fusion
  318.7 63.6 %while.11 = (s32[]{:T(128)}, f32[12,256]{1,0:T(8,128)S(1)}, bf16[12,4,256,128]{3,2,1,0:T(8,128)(2,1)}, s32[12]{0:T(128)S(1)}, bf16[32,4,128,128]{3,2,1,0:T(8,128)(2,1)}) while((s32[]{:T(128)}, f32[12,256]{1,0:T(8,128)S(1)}, bf16[12,4,256,128]{3,2,1,0:T(8,128)(2,1)}, s32[12]{0:T(128)S(1)}, bf16[32,4,128,128]{3,2,1,0:T(8,128)(2,1)}) %tuple.46), condition=%wide.region_2.3_spmd.clone, body=%wide.region_0.2_spmd.sunk.clone | while | flops 136183552 | bytes 3673207 | solution.py:90
  321.3 1.0 dynamic-slice_bitcast_fusion.4
  322.4 1.6 fusion.73
  326.5 1.0 dynamic-slice_bitcast_fusion.4
  327.7 1.6 fusion.73
  331.8 1.0 dynamic-slice_bitcast_fusion.4
  333.0 1.6 fusion.73
  337.1 1.0 dynamic-slice_bitcast_fusion.4
  338.3 1.6 fusion.73
  342.4 1.0 dynamic-slice_bitcast_fusion.4
  343.6 1.6 fusion.73
  347.7 1.0 dynamic-slice_bitcast_fusion.4
  348.9 1.6 fusion.73
  353.0 1.0 dynamic-slice_bitcast_fusion.4
  354.2 1.6 fusion.73
  358.3 1.0 dynamic-slice_bitcast_fusion.4
  359.5 1.6 fusion.73
  363.6 1.0 dynamic-slice_bitcast_fusion.4
  364.8 1.6 fusion.73
  368.9 1.0 dynamic-slice_bitcast_fusion.4
  370.1 1.6 fusion.73
  374.2 1.0 dynamic-slice_bitcast_fusion.4
  375.4 1.6 fusion.73
  379.5 1.0 dynamic-slice_bitcast_fusion.4
  380.7 1.6 fusion.73
  382.4 1.0 fusion.41
  383.8 1.4 copy.37
  385.2 1.3 dynamic-slice
  387.2 180.5 %all-reduce.5.cloned.1.call-done = f32[3,25,512]{1,0,2:T(4,128)} async-done(((f32[3,25,512]{1,0,2:T(4,128)}), f32[3,25,512]{1,0,2:T(4,128)}) %all-reduce.5.cloned.1.call-update) | async-done | bytes 153616
  567.7 0.9 constant_dynamic-slice_fusion.1
  568.6 5.2 collective-permute-start.1
  573.8 1.3 collective-permute-start
  575.1 1.4 collective-permute-done.1
  576.6 1.8 collective-permute-start.2
  578.3 1.1 collective-permute-start.3
  579.4 0.7 collective-permute-done.2
  580.1 1.9 collective-permute-done.3
  582.1 0.7 copy.41
  583.1 91.7 %all-gather.2.cloned.1.call-done = bf16[3,25,16,512]{1,2,0,3:T(8,128)(2,1)} async-done(((bf16[3,25,16,16]{1,2,0,3:T(8,128)(2,1)}), bf16[3,25,16,512]{1,2,0,3:T(8,128)(2,1)}) %all-gather.2.cloned.1.call-update) | async-done | bytes 1228816 | tf_op jit(solution)/shard_map/all_gather | solution.py:113
  674.7 6.5 copy.51
  681.3 3.4 gather_fusion.1
  684.7 2.2 multiply_reduce_fusion
  (85 shorter events, 11.3 us)
Async XLA Ops:
  16.6 11.5 %copy-start.3 = (s32[12,6]{0,1:T(8,128)S(1)}, s32[12,6]{0,1:T(8,128)}, u32[]{:S(2)}) copy-start(s32[12,6]{0,1:T(8,128)} %param.19) | copy-start | bytes 868
  16.6 289.8 %all-to-all-start = ((bf16[32,3,4,128,128]{4,3,2,1,0:T(8,128)(2,1)}), bf16[32,3,4,128,128]{4,3,2,1,0:T(8,128)(2,1)}, u32[]{:S(2)}, u32[]{:S(2)}) async-start(bf16[32,3,4,128,128]{4,3,2,1,0:T(8,128)(2,1)} %stack.14), calls=%async_computation | async-start | bytes 25165824 | tf_op jit(solution)/shard_map/all_to_all | solution.py:75
  27.4 540.3 %all-reduce.5.cloned.1.call-start = ((), (), s32[]{:S(2)}) async-start(), calls=%async_computation.2 | async-start | bytes 2097152
  314.0 4.7 copy-start.8
  318.7 63.6 %copy-start.5 = (s32[1,12]{1,0:T(1,128)S(1)}, s32[1,12]{1,0:T(1,128)}, u32[]{:S(2)}) copy-start(s32[1,12]{1,0:T(1,128)} %param.18) | copy-start | bytes 148
  318.7 63.7 %copy-start = (f32[12,6,256]{2,1,0:T(8,128)S(1)}, f32[12,6,256]{2,1,0:T(8,128)}, u32[]{:S(2)}) copy-start(f32[12,6,256]{2,1,0:T(8,128)} %param.21) | copy-start | bytes 221188
  318.7 63.7 %copy-start.6 = (bf16[12,6,25,256]{3,2,1,0:T(8,128)(2,1)S(1)}, bf16[12,6,25,256]{3,2,1,0:T(8,128)(2,1)}, u32[]{:S(2)}) copy-start(bf16[12,6,25,256]{3,2,1,0:T(8,128)(2,1)} %param.20) | copy-start | bytes 2764804
  382.4 2.8 copy-start.1
  383.8 192.8 %copy-start.4 = (f32[25,16]{0,1:T(8,128)S(1)}, f32[25,16]{0,1:T(8,128)}, u32[]{:S(2)}) copy-start(f32[25,16]{0,1:T(8,128)} %param.23) | copy-start | bytes 4804
  385.2 289.5 %all-gather.2.cloned.1.call-start = ((), (), s32[]{:S(2)}) async-start(), calls=%async_computation.1 | async-start | bytes 6488064 | tf_op jit(solution)/shard_map/all_gather | solution.py:113
  568.6 7.9 %collective-permute-start.1 = (f32[1,2,25,16]{2,1,3,0:T(2,128)S(1)}, f32[1,2,25,16]{2,1,3,0:T(2,128)S(1)}, u32[]{:S(2)}, u32[]{:S(2)}) collective-permute-start(f32[1,2,25,16]{2,1,3,0:T(2,128)S(1)} %maximum_bitcast_fusion), channel_id=1, source_target_pairs={{32,0},{64,32},{96,64},{128,96},{160,128},{192,160},{224,192},{256... | collective-permute-start | bytes 9608 | tf_op jit(solution)/shard_map/ppermute | solution.py:19
  573.8 2.7 collective-permute-start
  576.6 104.7 %copy-start.2 = (f32[25,16]{0,1:T(8,128)}, f32[25,16]{0,1:T(8,128)S(1)}, u32[]{:S(2)}) copy-start(f32[25,16]{0,1:T(8,128)S(1)} %fusion.47) | copy-start | bytes 4804
  576.6 3.5 collective-permute-start.2
  578.3 3.7 collective-permute-start.3
  674.7 10.0 %copy-start.7 = (f32[12,6,256]{2,1,0:T(8,128)S(1)}, f32[12,6,256]{2,1,0:T(8,128)}, u32[]{:S(2)}) copy-start(f32[12,6,256]{2,1,0:T(8,128)} %param.22) | copy-start | bytes 221188
Sparse Core Ops, SparseCore 0:
  385.3 182.3 all-reduce.4
  583.0 91.7 all-gather.1
